TPU v7x, 32 devices: a whole 2x2x4 slice. The times are simulated.
32 devices in a mesh: pipe: 16 (over z, y, core), tensor: 2 (over x).
Axes of the slice: x: 2, y: 2, z: 4, core: 2. Of those that a mesh axis runs over, the one named last changes fastest.
Arguments:
- tokens_x: bfloat16 [16, 384, 12288], P('pipe', None, 'tensor'), may hold values from -6 to 6
- queries: bfloat16 [16, 384, 12288], P('pipe', None, 'tensor'), may hold values from -120 to 120
- key_rows: bfloat16 [16, 384, 1024], P('pipe', None, 'tensor'), may hold values from -5 to 5
- out_grad: bfloat16 [16, 384, 12288], P('pipe', None, 'tensor'), may hold values from -4 to 4
- value_weight: bfloat16 [16, 12288, 1024], P('pipe', 'tensor'), may hold values from -0.0546875 to 0.0546875
- doc_starts: int32 [16, 384], P('pipe'), may hold values from 0 to 383, as said below
Outputs:
- query_grad: bfloat16 [16, 384, 12288], P('pipe', None, 'tensor')
- key_grad: bfloat16 [16, 384, 1024], P('pipe', None, 'tensor')
- weight_grad: bfloat16 [16, 12288, 1024], P('pipe', 'tensor')
- section_grad: bfloat16 [16, 384, 12288], P('pipe', None, 'tensor')
Inputs may be any that keep to these rules, and one draw needn't show every extreme that they name: doc_starts[s, 0] = 0, doc_starts[s, 383] = 383, doc_starts[s, i] <= i, and doc_starts[s, i] is either doc_starts[s, i - 1] or i.
All inputs are finite; a program needn't handle non-finite values.
Results may differ from a plain program's by a relative error of at most 0.012.
The roundings to bfloat16 on the way count: a program that leaves them out, or rounds other values in their place, can miss the bound.
Values may be sent and summed in bfloat16 or wider, within the bound.
A program may use at most 256 MiB of HBM per device.

v0:
```python
import jax
import jax.numpy as jnp
from jax import lax
from jax.sharding import PartitionSpec as P

HD = 128


def from_behind(value, axis, steps):
    count = lax.axis_size(axis)
    first, last = (max(0, -steps), min(count, count - steps))
    return lax.ppermute(value, axis, [(source, source + steps) for source in range(first, last)])


def attend(queries, key_rows, values, out_grad, doc_starts):
    length = queries.shape[0]
    kv_heads = key_rows.shape[1] // HD
    groups = queries.shape[1] // (kv_heads * HD)
    scaling = HD ** (-0.5)
    row_index = lax.broadcasted_iota(jnp.int32, (length, length), 0)
    col_index = lax.broadcasted_iota(jnp.int32, (length, length), 1)
    allowed = (col_index <= row_index) & (col_index >= doc_starts[:, None])
    query_heads = queries.reshape(length, kv_heads, groups, HD)
    key_heads = key_rows.reshape(length, kv_heads, HD)
    value_heads = values.reshape(length, kv_heads, HD)
    grad_heads = out_grad.reshape(length, kv_heads, groups, HD)

    def one_group(query_g, key_g, value_g, grad_g):
        scores = (
            jnp.einsum("igd,jd->gij", query_g, key_g, preferred_element_type=jnp.float32) * scaling
        )
        scores = jnp.where(allowed[None], scores, -1e30)
        top_score = jnp.max(scores, axis=2, keepdims=True)
        expo = jnp.exp(scores - top_score)
        probs = expo / jnp.sum(expo, axis=2, keepdims=True)
        probs_low = probs.astype(jnp.bfloat16)
        attended = jnp.einsum("gij,jd->igd", probs_low, value_g, preferred_element_type=jnp.float32)
        delta = jnp.sum(grad_g.astype(jnp.float32) * attended, axis=2)
        grad_probs = jnp.einsum("igd,jd->gij", grad_g, value_g, preferred_element_type=jnp.float32)
        grad_scores = probs * (grad_probs - delta.T[:, :, None])
        scaled_low = (grad_scores * scaling).astype(jnp.bfloat16)
        grad_query = jnp.einsum(
            "gij,jd->igd", scaled_low, key_g, preferred_element_type=jnp.float32
        ).astype(jnp.bfloat16)
        grad_key = jnp.einsum(
            "gij,igd->jd", scaled_low, query_g, preferred_element_type=jnp.float32
        ).astype(jnp.bfloat16)
        grad_value = jnp.einsum(
            "gij,igd->jd", probs_low, grad_g, preferred_element_type=jnp.float32
        ).astype(jnp.bfloat16)
        return (grad_query, grad_key, grad_value)

    grad_query, grad_key, grad_value = jax.vmap(
        one_group, in_axes=(1, 1, 1, 1), out_axes=(1, 1, 1)
    )(query_heads, key_heads, value_heads, grad_heads)
    return (
        grad_query.reshape(length, -1),
        grad_key.reshape(length, -1),
        grad_value.reshape(length, -1),
    )


def shards(tokens_x, queries, key_rows, out_grad, value_weight, doc_starts):
    inputs = tokens_x[0]
    query_s = queries[0]
    key_s = key_rows[0]
    grad_s = out_grad[0]
    panel = value_weight[0]
    starts_s = doc_starts[0]
    weight_cols = lax.all_to_all(panel, "tensor", split_axis=1, concat_axis=0, tiled=True)
    inputs_all = lax.all_gather(inputs, "tensor", axis=1, tiled=True)
    values = jnp.dot(inputs_all, weight_cols, preferred_element_type=jnp.float32).astype(
        jnp.bfloat16
    )
    grad_query, grad_key, grad_value = attend(query_s, key_s, values, grad_s, starts_s)
    grad_cols = lax.dot_general(
        inputs_all, grad_value, (((0,), (0,)), ((), ())), preferred_element_type=jnp.float32
    ).astype(jnp.bfloat16)
    weight_grad = lax.all_to_all(grad_cols, "tensor", split_axis=0, concat_axis=1, tiled=True)
    terms = lax.dot_general(
        grad_value, weight_cols, (((1,), (1,)), ((), ())), preferred_element_type=jnp.float32
    )
    input_grad = lax.psum_scatter(terms, "tensor", scatter_dimension=1, tiled=True).astype(
        jnp.bfloat16
    )
    received = from_behind(input_grad, "pipe", -1)
    return (grad_query[None], grad_key[None], weight_grad[None], received[None])


def solution(mesh):
    placed = (
        P("pipe", None, "tensor"),
        P("pipe", None, "tensor"),
        P("pipe", None, "tensor"),
        P("pipe", None, "tensor"),
        P("pipe", "tensor", None),
        P("pipe", None),
    )
    return jax.shard_map(
        shards,
        mesh=mesh,
        in_specs=placed,
        out_specs=(
            P("pipe", None, "tensor"),
            P("pipe", None, "tensor"),
            P("pipe", "tensor", None),
            P("pipe", None, "tensor"),
        ),
        check_vma=False,
    )
```

profile of v0, /device:TPU:1, one launch (start us, length us, event | category | flops | bytes accessed | tf_op | source)
XLA Modules:
  0.0 730.0 jit_solution(1472528996618862194)
XLA Ops:
  7.2 0.0 all-gather.3.cloned.1.call-start
  7.2 0.7 all-gather.3.cloned.1.call-update
  7.9 17.1 %copy.60 = bf16[1,6144,1024]{1,2,0:T(8,128)(2,1)} copy(bf16[1,6144,1024]{2,1,0:T(8,128)(2,1)} %param.10) | data formatting | bytes 25165824 | tf_op args[4]
  25.0 0.0 copy-start.2
  25.0 9.1 %all-to-all-start = ((bf16[6144,2,512]{0,2,1:T(8,128)(2,1)}), bf16[6144,2,512]{0,2,1:T(8,128)(2,1)}, u32[]{:S(2)}, u32[]{:S(2)}) async-start(bf16[6144,2,512]{0,2,1:T(8,128)(2,1)} %bitcast.91), calls=%async_computation | async-start | bytes 25165824 | tf_op jit(solution)/shard_map/all_to_all | solution.py:70
  34.1 0.0 copy-start.3
  34.1 0.0 reduce-scatter.2.cloned.1.call-start
  34.1 0.0 copy-done.2
  34.2 0.1 reshape_squeeze.9
  34.3 0.3 copy.82
  34.5 6.7 copy.57
  41.2 6.6 copy.62
  47.8 0.0 copy-done.3
  47.8 0.1 fusion.20
  47.9 16.4 %fusion.23 = (f32[4,12,384]{2,1,0:T(8,128)S(1)}, f32[4,12,384,384]{2,3,1,0:T(8,128)}) fusion(pred[384,384]{0,1:T(8,128)(4,1)S(1)} %fusion.20, bf16[384,4,128,1]{0,2,3,1:T(8,128)(2,1)S(1)} %copy.82, bf16[384,4,12,128]{0,3,2,1:T(8,128)(2,1)} %bitcast.95), kind=kOutput, calls=%fused_computation.32 | convolution fusion | flops 1840251264 | bytes 33644544 | tf_op jit(solution)/shard_map/vmap()/sub | solution.py:34
  64.3 0.0 copy-start.1
  64.3 11.5 %fusion.8 = bf16[4,12,384,384]{2,3,1,0:T(8,128)(2,1)S(1)} fusion(f32[4,12,384,384]{2,3,1,0:T(8,128)} %get-tuple-element.21, f32[4,12,384]{2,1,0:T(8,128)S(1)} %get-tuple-element.20), kind=kLoop, calls=%fused_computation.14 | loop fusion | flops 14155776 | bytes 42541056 | tf_op jit(solution)/shard_map/vmap()/convert_element_type | solution.py:36
  75.8 0.0 copy-start
  75.8 5.0 copy-done
  80.8 0.0 copy-done.1
  80.9 4.2 fusion.16
  85.0 179.3 %all-to-all-done = bf16[6144,2,512]{0,2,1:T(8,128)(2,1)} async-done(((bf16[6144,2,512]{0,2,1:T(8,128)(2,1)}), bf16[6144,2,512]{0,2,1:T(8,128)(2,1)}, u32[]{:S(2)}, u32[]{:S(2)}) %all-to-all-start) | async-done | bytes 12582944 | tf_op jit(solution)/shard_map/all_to_all | solution.py:70
  264.3 16.6 %copy.61 = bf16[2,6144,512]{2,1,0:T(8,128)(2,1)} copy(bf16[2,6144,512]{1,2,0:T(8,128)(2,1)} %bitcast.5) | data formatting | bytes 25165824 | tf_op jit(solution)/shard_map/all_to_all | solution.py:70
  280.9 20.1 %fusion.24 = f32[384,12288]{1,0:T(8,128)} fusion(bf16[384,512]{0,1:T(8,128)(2,1)S(1)} %bitcast.99, bf16[12288,512]{1,0:T(8,128)(2,1)} %bitcast.88), kind=kOutput, calls=%fused_computation.33 | convolution fusion | flops 4831838208 | bytes 31850496 | tf_op jit(solution)/shard_map/dot_general | solution.py:80
  301.0 0.0 reduce-scatter.2.cloned.1.call-update
  301.0 0.0 all-gather.3.cloned.1.call-done
  301.1 10.9 %fusion.17 = bf16[384,512]{1,0:T(8,128)(2,1)S(1)} fusion(bf16[12288,512]{1,0:T(8,128)(2,1)} %bitcast.89, bf16[1,384,12288]{2,1,0:T(8,128)(2,1)} %all-gather.3.cloned.1.call-done), kind=kOutput, calls=%fused_computation.26 | convolution fusion | flops 4832034816 | bytes 22413312 | tf_op jit(solution)/shard_map/dot_general | solution.py:72
  312.0 0.1 reshape.26
  312.1 0.3 copy.79
  312.4 10.8 %convolution_convert_fusion = bf16[512,12288]{1,0:T(8,128)(2,1)S(1)} fusion(bf16[384,512]{0,1:T(8,128)(2,1)S(1)} %bitcast.100, bf16[1,384,12288]{2,1,0:T(8,128)(2,1)} %all-gather.3.cloned.1.call-done), kind=kOutput, calls=%fused_computation.8 | convolution fusion | flops 4838129664 | bytes 22413312 | tf_op jit(solution)/shard_map/dot_general | solution.py:76
  323.2 5.1 copy.97
  328.3 8.3 %all-to-all-start.1 = ((bf16[2,6144,512]{1,2,0:T(8,128)(2,1)}), bf16[2,6144,512]{1,2,0:T(8,128)(2,1)}, u32[]{:S(2)}, u32[]{:S(2)}) async-start(bf16[2,6144,512]{1,2,0:T(8,128)(2,1)} %bitcast.90), calls=%async_computation.1 | async-start | bytes 25165824 | tf_op jit(solution)/shard_map/all_to_all | solution.py:79
  336.6 9.0 %fusion.9 = f32[4,384,12]{1,2,0:T(8,128)S(1)} fusion(bf16[384,4,12,128]{0,3,2,1:T(8,128)(2,1)} %bitcast.92, bf16[384,4,128,1]{0,2,3,1:T(8,128)(2,1)S(1)} %copy.79, bf16[4,12,384,384]{2,3,1,0:T(8,128)(2,1)} %copy-done), kind=kOutput, calls=%fused_computation.16 | convolution fusion | flops 1818998784 | bytes 19341312 | tf_op jit(solution)/shard_map/vmap(gij,jd->igd)/dot_general | solution.py:37
  345.6 302.1 %reduce-scatter.2.cloned.1.call-done = f32[384,6144]{1,0:T(8,128)} async-done(((f32[384,12288]{1,0:T(8,128)}), f32[384,6144]{1,0:T(8,128)}) %reduce-scatter.2.cloned.1.call-update) | async-done | bytes 9437200 | tf_op jit(solution)/shard_map/reduce_scatter | solution.py:83
  647.7 6.5 convert_element_type.51
  654.2 2.6 collective-permute-start
  656.8 18.7 %fusion.3 = bf16[4,12,384,384]{2,3,1,0:T(8,128)(2,1)} fusion(f32[4,12,384]{2,1,0:T(8,128)S(1)} %bitcast.104, bf16[384,4,128,1]{0,2,3,1:T(8,128)(2,1)S(1)} %copy.79, bf16[384,4,12,128]{0,3,2,1:T(8,128)(2,1)} %bitcast.93, f32[4,12,384,384]{2,3,1,0:T(8,128)} %get-tuple-element.21, f32[4,12,384]{2,1,0:T(8,128)S(1)} %get-tuple-element.20), kind=kOutput, calls=%fused_computation.4 | convolution fusion | flops 1847328768 | bytes 47726592 | tf_op jit(solution)/shard_map/vmap(igd,jd->gij)/dot_general | solution.py:39
  675.6 9.9 %convolution_convert_fusion.1 = bf16[4,12,384,128]{2,3,1,0:T(8,128)(2,1)} fusion(bf16[384,4,128,1]{0,2,3,1:T(8,128)(2,1)S(1)} %copy.82, bf16[4,12,384,384]{2,3,1,0:T(8,128)(2,1)} %fusion.3), kind=kOutput, calls=%fused_computation.21 | convolution fusion | flops 1814298624 | bytes 19267584 | tf_op jit(solution)/shard_map/vmap(gij,jd->igd)/dot_general | solution.py:42
  685.5 6.6 copy.72
  692.1 8.4 %fusion.15 = bf16[4,384,128]{1,2,0:T(8,128)(2,1)S(1)} fusion(bf16[4,12,384,384]{2,3,1,0:T(8,128)(2,1)} %fusion.3, bf16[384,4,12,128]{0,3,2,1:T(8,128)(2,1)} %bitcast.96), kind=kOutput, calls=%fused_computation.24 | convolution fusion | flops 1812135936 | bytes 19267584 | tf_op jit(solution)/shard_map/vmap(gij,igd->jd)/dot_general | solution.py:45
  700.5 0.9 copy.73
  701.5 0.0 all-to-all-done.1
  701.5 16.6 %copy.74 = bf16[1,6144,1024]{2,1,0:T(8,128)(2,1)} copy(bf16[1,6144,1024]{1,2,0:T(8,128)(2,1)} %bitcast.27) | data formatting | bytes 25165824
  718.1 0.0 collective-permute-done
  718.1 5.1 copy.99
  (1 shorter events, 0.0 us)
Async XLA Ops:
  7.2 293.9 %all-gather.3.cloned.1.call-start = ((), (), s32[]{:S(2)}) async-start(), calls=%async_computation.4 | async-start | bytes 14155776 | tf_op jit(solution)/shard_map/all_gather | solution.py:71
  25.0 9.2 %copy-start.2 = (bf16[1,384,512]{2,1,0:T(8,128)(2,1)S(1)}, bf16[1,384,512]{2,1,0:T(8,128)(2,1)}, u32[]{:S(2)}) copy-start(bf16[1,384,512]{2,1,0:T(8,128)(2,1)} %param.8) | copy-start | bytes 1179652
  25.0 239.3 %all-to-all-start = ((bf16[6144,2,512]{0,2,1:T(8,128)(2,1)}), bf16[6144,2,512]{0,2,1:T(8,128)(2,1)}, u32[]{:S(2)}, u32[]{:S(2)}) async-start(bf16[6144,2,512]{0,2,1:T(8,128)(2,1)} %bitcast.91), calls=%async_computation | async-start | bytes 25165824 | tf_op jit(solution)/shard_map/all_to_all | solution.py:70
  34.1 13.7 %copy-start.3 = (s32[1,384]{1,0:T(1,128)S(1)}, s32[1,384]{1,0:T(1,128)}, u32[]{:S(2)}) copy-start(s32[1,384]{1,0:T(1,128)} %param.11) | copy-start | bytes 4612
  34.1 613.6 %reduce-scatter.2.cloned.1.call-start = ((), (), s32[]{:S(2)}) async-start(), calls=%async_computation.3 | async-start | bytes 28311552 | tf_op jit(solution)/shard_map/reduce_scatter | solution.py:83
  64.3 16.5 %copy-start.1 = (bf16[1,384,6144]{1,2,0:T(8,128)(2,1)S(1)}, bf16[1,384,6144]{1,2,0:T(8,128)(2,1)}, u32[]{:S(2)}) copy-start(bf16[1,384,6144]{1,2,0:T(8,128)(2,1)} %copy.62) | copy-start | bytes 14155780
  75.8 5.0 copy-start
  328.3 373.2 %all-to-all-start.1 = ((bf16[2,6144,512]{1,2,0:T(8,128)(2,1)}), bf16[2,6144,512]{1,2,0:T(8,128)(2,1)}, u32[]{:S(2)}, u32[]{:S(2)}) async-start(bf16[2,6144,512]{1,2,0:T(8,128)(2,1)} %bitcast.90), calls=%async_computation.1 | async-start | bytes 25165824 | tf_op jit(solution)/shard_map/all_to_all | solution.py:79
  654.2 63.8 %collective-permute-start = (bf16[384,6144]{1,0:T(8,128)(2,1)}, bf16[384,6144]{1,0:T(8,128)(2,1)}, u32[]{:S(2)}, u32[]{:S(2)}) collective-permute-start(bf16[384,6144]{1,0:T(8,128)(2,1)} %convert_element_type.51), channel_id=1, source_target_pairs={{2,0},{4,2},{6,4},{8,6},{10,8},{12,10},{14,12},{16,14},{18,16},{20... | collective-permute-start | bytes 14155784 | tf_op jit(solution)/shard_map/ppermute | solution.py:12
Sparse Core Ops, SparseCore 0:
  9.6 211.6 all-gather.2
  301.2 346.4 reduce-scatter.1
where the time goes:
time: 733 us; the launch traced here: 730 us
  waiting for transfers between devices  482 us (66%)
  matrix products  108 us (15%)
  local copies, waits for them, and re-layouts  87.1 us (12%)
  starting transfers between devices  20.1 us (3%)
  other arithmetic  18.1 us (2%)
  between operations  14.2 us (2%)
    reduce_scatter x1, waiting for transfers between devices, shards(): lax.psum_scatter(terms, 'tensor', scatter_dimension=1, tiled=True)  302 us
    all_to_all x1, waiting for transfers between devices, shards(): lax.all_to_all(panel, 'tensor', split_axis=1, concat_axis=0, tiled=True)  179 us
    unnamed x15, local copies, waits for them, and re-layouts  64.6 us
    dot_general x1, matrix products, shards(): lax.dot_general(grad_value, weight_cols, (((1,), (1,)), ((), ())), prefer...  20.1 us
    dot_general x1, matrix products, one_group(): jnp.einsum('igd,jd->gij', grad_g, value_g, preferred_element_type=jnp.flo...  18.7 us
    all_to_all x1, local copies, waits for them, and re-layouts, shards(): lax.all_to_all(panel, 'tensor', split_axis=1, concat_axis=0, tiled=True)  16.6 us
    sub x1, matrix products, one_group(): expo = jnp.exp(scores - top_score)  16.4 us
  transfers between devices with their start and end apart: 5, of which 2 were waited for; matrix products, arithmetic and copies ran while one was open for 28% of the time, Pallas kernels for 0%

commit v1 on v0

--- a/solution.py
+++ b/solution.py
@@ -60,6 +60,35 @@
     )
 
 
+def sum_columns(terms, axis):
+    count = lax.axis_size(axis)
+    me = lax.axis_index(axis)
+    width = terms.shape[1] // count
+    total = lax.dynamic_slice_in_dim(terms, me * width, width, axis=1)
+    for step in range(1, count):
+        target = lax.rem(me + step, count)
+        block = lax.dynamic_slice_in_dim(terms, target * width, width, axis=1)
+        total = total + lax.ppermute(
+            block, axis, [(source, (source + step) % count) for source in range(count)]
+        )
+    return total
+
+
+def join_columns(block, axis):
+    count = lax.axis_size(axis)
+    me = lax.axis_index(axis)
+    width = block.shape[1]
+    whole = jnp.zeros((block.shape[0], width * count), block.dtype)
+    whole = lax.dynamic_update_slice_in_dim(whole, block, me * width, axis=1)
+    for step in range(1, count):
+        origin = lax.rem(me + count - step, count)
+        came = lax.ppermute(
+            block, axis, [(source, (source + step) % count) for source in range(count)]
+        )
+        whole = lax.dynamic_update_slice_in_dim(whole, came, origin * width, axis=1)
+    return whole
+
+
 def shards(tokens_x, queries, key_rows, out_grad, value_weight, doc_starts):
     inputs = tokens_x[0]
     query_s = queries[0]
@@ -67,23 +96,17 @@
     grad_s = out_grad[0]
     panel = value_weight[0]
     starts_s = doc_starts[0]
-    weight_cols = lax.all_to_all(panel, "tensor", split_axis=1, concat_axis=0, tiled=True)
-    inputs_all = lax.all_gather(inputs, "tensor", axis=1, tiled=True)
-    values = jnp.dot(inputs_all, weight_cols, preferred_element_type=jnp.float32).astype(
-        jnp.bfloat16
-    )
+    terms = jnp.dot(inputs, panel, preferred_element_type=jnp.float32)
+    values = sum_columns(terms, "tensor").astype(jnp.bfloat16)
     grad_query, grad_key, grad_value = attend(query_s, key_s, values, grad_s, starts_s)
-    grad_cols = lax.dot_general(
-        inputs_all, grad_value, (((0,), (0,)), ((), ())), preferred_element_type=jnp.float32
+    grad_all = join_columns(grad_value, "tensor")
+    input_grad = lax.dot_general(
+        grad_all, panel, (((1,), (1,)), ((), ())), preferred_element_type=jnp.float32
     ).astype(jnp.bfloat16)
-    weight_grad = lax.all_to_all(grad_cols, "tensor", split_axis=0, concat_axis=1, tiled=True)
-    terms = lax.dot_general(
-        grad_value, weight_cols, (((1,), (1,)), ((), ())), preferred_element_type=jnp.float32
-    )
-    input_grad = lax.psum_scatter(terms, "tensor", scatter_dimension=1, tiled=True).astype(
-        jnp.bfloat16
-    )
     received = from_behind(input_grad, "pipe", -1)
+    weight_grad = lax.dot_general(
+        inputs, grad_all, (((0,), (0,)), ((), ())), preferred_element_type=jnp.float32
+    ).astype(jnp.bfloat16)
     return (grad_query[None], grad_key[None], weight_grad[None], received[None])
 
 

time: 733 us -> 171 us (0.23)
  waiting for transfers between devices: 482 us -> 0.01 us
  local copies, waits for them, and re-layouts: 87.1 us -> 45.4 us
  starting transfers between devices: 20.1 us -> 5.33 us
  between operations: 14.2 us -> 0.84 us
    reduce_scatter x1 -> x0, waiting for transfers between devices: 302 us -> none  [shards(): lax.psum_scatter(terms, 'tensor', scatter_dimension=1, tiled=True)]
    all_to_all x2 -> x0, waiting for transfers between devices: 179 us -> none  [the longest x1 179 us: shards(): lax.all_to_all(panel, 'tensor', split_axis=1, concat_axis=0, tiled=True)]
    unnamed x15 -> x18, local copies, waits for them, and re-layouts: 64.6 us -> 42.5 us
    all_to_all x2 -> x0, local copies, waits for them, and re-layouts: 21.7 us -> none  [the longest x1 16.6 us: shards(): lax.all_to_all(panel, 'tensor', split_axis=1, concat_axis=0, tiled=True)]
    all_to_all x2 -> x0, starting transfers between devices: 17.4 us -> none  [the longest x1 9.09 us: shards(): lax.all_to_all(panel, 'tensor', split_axis=1, concat_axis=0, tiled=True)]
  transfers between devices with their start and end apart: 5 -> 3, of which waited for: 2 -> 0; matrix products, arithmetic and copies ran while one was open for 28% -> 65% of each run, Pallas kernels for 0% -> 0%
where the time goes in v1:
time: 171 us; the launch traced here: 168 us
  matrix products  103 us (60%)
  local copies, waits for them, and re-layouts  45.4 us (27%)
  other arithmetic  13.5 us (8%)
  starting transfers between devices  5.33 us (3%)
    unnamed x18, local copies, waits for them, and re-layouts  42.5 us
    dot_general x1, matrix products, shards(): lax.dot_general(grad_all, panel, (((1,), (1,)), ((), ())), preferred_elem...  19.1 us
    dot_general x1, matrix products, one_group(): jnp.einsum('igd,jd->gij', grad_g, value_g, preferred_element_type=jnp.flo...  16.9 us
    sub x1, matrix products, one_group(): expo = jnp.exp(scores - top_score)  16.4 us
    convert_element_type x1, other arithmetic, one_group(): probs_low = probs.astype(jnp.bfloat16)  11.4 us
    dot_general x1, matrix products, one_group(): jnp.einsum('gij,jd->igd', scaled_low, key_g, preferred_element_type=jnp.f...  9.83 us
    dot_general x1, matrix products, shards(): lax.dot_general(inputs, grad_all, (((0,), (0,)), ((), ())), preferred_ele...  9.53 us
    dot_general x1, matrix products, shards(): terms = jnp.dot(inputs, panel, preferred_element_type=jnp.float32)  9.45 us
  transfers between devices with their start and end apart: 3, of which 0 were waited for; matrix products, arithmetic and copies ran while one was open for 65% of the time, Pallas kernels for 0%

profile of v1, /device:TPU:1, one launch (start us, length us, event | category | flops | bytes accessed | tf_op | source)
XLA Modules:
  0.0 168.1 jit_solution(8863863233504491356)
XLA Ops:
  0.6 0.7 reduce
  1.3 0.1 fusion.23
  1.4 1.1 reshape_squeeze.9
  2.5 0.3 copy.47
  2.8 6.7 %copy.25 = bf16[1,384,6144]{1,2,0:T(8,128)(2,1)} copy(bf16[1,384,6144]{2,1,0:T(8,128)(2,1)} %param.7) | data formatting | bytes 9437184 | tf_op args[1]
  9.5 6.6 %copy.28 = bf16[1,384,6144]{1,2,0:T(8,128)(2,1)} copy(bf16[1,384,6144]{2,1,0:T(8,128)(2,1)} %param.9) | data formatting | bytes 9437184 | tf_op args[3]
  16.1 16.4 %fusion.26 = (f32[4,12,384]{2,1,0:T(8,128)S(1)}, f32[4,12,384,384]{2,3,1,0:T(8,128)}) fusion(pred[384,384]{0,1:T(8,128)(4,1)S(1)} %fusion.23, bf16[384,4,128,1]{0,2,3,1:T(8,128)(2,1)S(1)} %copy.47, bf16[384,4,12,128]{0,3,2,1:T(8,128)(2,1)} %bitcast.89), kind=kOutput, calls=%fused_computation.38 | convolution fusion | flops 1840251264 | bytes 33644544 | tf_op jit(solution)/shard_map/vmap()/sub | solution.py:34
  32.5 0.0 copy-start.1
  32.5 11.4 %fusion.12 = bf16[4,12,384,384]{2,3,1,0:T(8,128)(2,1)S(1)} fusion(f32[4,12,384,384]{2,3,1,0:T(8,128)} %get-tuple-element.13, f32[4,12,384]{2,1,0:T(8,128)S(1)} %get-tuple-element.12), kind=kLoop, calls=%fused_computation.17 | loop fusion | flops 14155776 | bytes 42541056 | tf_op jit(solution)/shard_map/vmap()/convert_element_type | solution.py:36
  43.9 0.0 copy-start
  43.9 0.0 copy-done.1
  43.9 4.2 %fusion.22 = bf16[4,384,128]{1,2,0:T(8,128)(2,1)S(1)} fusion(bf16[4,12,384,384]{2,3,1,0:T(8,128)(2,1)S(1)} %fusion.12, bf16[384,4,12,128]{0,3,2,1:T(8,128)(2,1)S(1)} %bitcast.85), kind=kOutput, calls=%fused_computation.28 | convolution fusion | flops 1812135936 | bytes 19267584 | tf_op jit(solution)/shard_map/vmap(gij,igd->jd)/dot_general | solution.py:48
  48.1 2.1 %collective-permute-start.1 = (bf16[384,512]{0,1:T(8,128)(2,1)S(1)}, bf16[384,512]{0,1:T(8,128)(2,1)S(1)}, u32[]{:S(2)}, u32[]{:S(2)}) collective-permute-start(bf16[384,512]{0,1:T(8,128)(2,1)S(1)} %bitcast.95), channel_id=1, source_target_pairs={{0,1},{1,0},{2,3},{3,2},{4,5},{5,4},{6,7},{7,6},{8,9},{9,8},{10,11... | collective-permute-start | bytes 1179656 | tf_op jit(solution)/shard_map/ppermute | solution.py:85
  50.2 9.4 %fusion.10 = f32[384,1024]{1,0:T(8,128)S(1)} fusion(bf16[1,6144,1024]{2,1,0:T(8,128)(2,1)} %param.10, bf16[1,384,6144]{2,1,0:T(8,128)(2,1)} %param.6), kind=kOutput, calls=%fused_computation.14 | convolution fusion | flops 4831838208 | bytes 18874368 | tf_op jit(solution)/shard_map/dot_general | solution.py:99
  59.6 0.0 copy-done
  59.7 1.0 constant_dynamic-slice_fusion
  60.6 0.4 collective-permute-start
  61.0 0.0 slice-start.2
  61.0 0.1 broadcast_in_dim.27
  61.1 0.1 constant_dynamic-update-slice_fusion.1
  61.1 0.0 collective-permute-done.1
  61.2 0.1 constant_dynamic-update-slice_fusion
  61.2 0.0 slice-start.3
  61.2 19.1 %fusion.14 = bf16[384,6144]{1,0:T(8,128)(2,1)} fusion(bf16[384,1024]{0,1:T(8,128)(2,1)S(1)} %constant_dynamic-update-slice_fusion, bf16[1,6144,1024]{2,1,0:T(8,128)(2,1)} %param.10), kind=kOutput, calls=%fused_computation.20 | convolution fusion | flops 4834197504 | bytes 18087936 | tf_op jit(solution)/shard_map/dot_general | solution.py:103
  80.3 2.8 %collective-permute-start.2 = (bf16[384,6144]{1,0:T(8,128)(2,1)}, bf16[384,6144]{1,0:T(8,128)(2,1)}, u32[]{:S(2)}, u32[]{:S(2)}) collective-permute-start(bf16[384,6144]{1,0:T(8,128)(2,1)} %fusion.14), channel_id=1, source_target_pairs={{2,0},{4,2},{6,4},{8,6},{10,8},{12,10},{14,12},{16,14},{18,16},{20... | collective-permute-start | bytes 14155784 | tf_op jit(solution)/shard_map/ppermute | solution.py:12
  83.2 0.0 slice-done.2
  83.2 0.0 slice-done.3
  83.2 9.5 %convert_bitcast_fusion = bf16[1,6144,1024]{1,2,0:T(8,128)(2,1)} fusion(bf16[384,1024]{0,1:T(8,128)(2,1)S(1)} %constant_dynamic-update-slice_fusion, bf16[1,384,6144]{2,1,0:T(8,128)(2,1)S(1)} %bitcast.99), kind=kOutput, calls=%fused_computation.16 | convolution fusion | flops 4838129664 | bytes 18087936 | tf_op jit(solution)/shard_map/dot_general | solution.py:107
  92.7 16.6 %copy.39 = bf16[1,6144,1024]{2,1,0:T(8,128)(2,1)} copy(bf16[1,6144,1024]{1,2,0:T(8,128)(2,1)} %convert_bitcast_fusion) | data formatting | bytes 25165824
  109.3 0.0 slice-start
  109.3 0.0 collective-permute-done
  109.3 1.3 add_convert_fusion
  110.6 0.1 reshape.18
  110.7 0.3 copy.44
  111.0 0.0 slice-start.1
  111.0 9.2 %fusion.13 = f32[4,384,12]{1,2,0:T(8,128)S(1)} fusion(bf16[384,4,12,128]{0,3,2,1:T(8,128)(2,1)} %bitcast.84, bf16[384,4,128,1]{0,2,3,1:T(8,128)(2,1)S(1)} %copy.44, bf16[4,12,384,384]{2,3,1,0:T(8,128)(2,1)} %copy-done), kind=kOutput, calls=%fused_computation.19 | convolution fusion | flops 1818998784 | bytes 19341312 | tf_op jit(solution)/shard_map/vmap(gij,jd->igd)/dot_general | solution.py:37
  120.2 0.0 slice-done
  120.2 0.0 slice-done.1
  120.2 16.9 %fusion.3 = bf16[4,12,384,384]{2,3,1,0:T(8,128)(2,1)} fusion(f32[4,12,384]{2,1,0:T(8,128)S(1)} %bitcast.97, bf16[384,4,128,1]{0,2,3,1:T(8,128)(2,1)S(1)} %copy.44, bf16[384,4,12,128]{0,3,2,1:T(8,128)(2,1)S(1)} %bitcast.88, f32[4,12,384,384]{2,3,1,0:T(8,128)} %get-tuple-element.13, f32[4,12,384]{2,1,0:T(8,128)S(1)} %get-tuple-element.12), kind=kOutput, calls=%fused_computation.4 | convolution fusion | flops 1847328768 | bytes 47726592 | tf_op jit(solution)/shard_map/vmap(igd,jd->gij)/dot_general | solution.py:39
  137.2 9.8 %convolution_convert_fusion = bf16[4,12,384,128]{2,3,1,0:T(8,128)(2,1)} fusion(bf16[384,4,128,1]{0,2,3,1:T(8,128)(2,1)S(1)} %copy.47, bf16[4,12,384,384]{2,3,1,0:T(8,128)(2,1)} %fusion.3), kind=kOutput, calls=%fused_computation.24 | convolution fusion | flops 1814298624 | bytes 19267584 | tf_op jit(solution)/shard_map/vmap(gij,jd->igd)/dot_general | solution.py:42
  147.0 6.6 %copy.37 = bf16[1,384,6144]{2,1,0:T(8,128)(2,1)} copy(bf16[1,384,6144]{1,2,0:T(8,128)(2,1)} %bitcast.91) | data formatting | bytes 9437184
  153.6 8.4 %fusion.21 = bf16[4,384,128]{1,2,0:T(8,128)(2,1)S(1)} fusion(bf16[4,12,384,384]{2,3,1,0:T(8,128)(2,1)} %fusion.3, bf16[384,4,12,128]{0,3,2,1:T(8,128)(2,1)} %bitcast.90), kind=kOutput, calls=%fused_computation.27 | convolution fusion | flops 1812135936 | bytes 19267584 | tf_op jit(solution)/shard_map/vmap(gij,igd->jd)/dot_general | solution.py:45
  162.1 0.9 copy.38
  163.0 0.0 collective-permute-done.2
  163.0 5.1 %copy.63 = bf16[1,384,6144]{2,1,0:T(8,128)(2,1)} copy(bf16[1,384,6144]{2,1,0:T(8,128)(2,1)} %bitcast.26) | data formatting | bytes 9437184
  (2 shorter events, 0.0 us)
Async XLA Ops:
  32.5 11.4 %copy-start.1 = (bf16[1,384,6144]{1,2,0:T(8,128)(2,1)S(1)}, bf16[1,384,6144]{1,2,0:T(8,128)(2,1)}, u32[]{:S(2)}) copy-start(bf16[1,384,6144]{1,2,0:T(8,128)(2,1)} %copy.28) | copy-start | bytes 14155780
  43.9 15.8 %copy-start = (bf16[4,12,384,384]{2,3,1,0:T(8,128)(2,1)}, bf16[4,12,384,384]{2,3,1,0:T(8,128)(2,1)S(1)}, u32[]{:S(2)}) copy-start(bf16[4,12,384,384]{2,3,1,0:T(8,128)(2,1)S(1)} %fusion.12) | copy-start | bytes 42467332
  48.1 13.1 %collective-permute-start.1 = (bf16[384,512]{0,1:T(8,128)(2,1)S(1)}, bf16[384,512]{0,1:T(8,128)(2,1)S(1)}, u32[]{:S(2)}, u32[]{:S(2)}) collective-permute-start(bf16[384,512]{0,1:T(8,128)(2,1)S(1)} %bitcast.95), channel_id=1, source_target_pairs={{0,1},{1,0},{2,3},{3,2},{4,5},{5,4},{6,7},{7,6},{8,9},{9,8},{10,11... | collective-permute-start | bytes 1179656 | tf_op jit(solution)/shard_map/ppermute | solution.py:85
  60.6 48.7 %collective-permute-start = (f32[384,512]{1,0:T(8,128)}, f32[384,512]{1,0:T(8,128)}, u32[]{:S(2)}, u32[]{:S(2)}) collective-permute-start(f32[384,512]{1,0:T(8,128)} %constant_dynamic-slice_fusion), channel_id=1, source_target_pairs={{0,1},{1,0},{2,3},{3,2},{4,5},{5,4},{6,7},{7,6},{8,9},{9,8},{10,11... | collective-permute-start | bytes 2359304 | tf_op jit(solution)/shard_map/ppermute | solution.py:71
  61.0 22.2 %slice-start.2 = ((s8[4718592]{0:T(1024)(128)(4,1)}), s8[4194304]{0:T(1024)(128)(4,1)S(1)}, s32[]{:S(2)}) async-start(s8[4718592]{0:T(1024)(128)(4,1)} %bitcast.98), calls=%async_computation.2 | async-start | bytes 8388608
  61.2 22.0 %slice-start.3 = ((s8[4718592]{0:T(1024)(128)(4,1)}), s8[524288]{0:T(1024)(128)(4,1)S(1)}, s32[]{:S(2)}) async-start(s8[4718592]{0:T(1024)(128)(4,1)} %bitcast.98), calls=%async_computation.3 | async-start | bytes 1048576
  80.3 82.7 %collective-permute-start.2 = (bf16[384,6144]{1,0:T(8,128)(2,1)}, bf16[384,6144]{1,0:T(8,128)(2,1)}, u32[]{:S(2)}, u32[]{:S(2)}) collective-permute-start(bf16[384,6144]{1,0:T(8,128)(2,1)} %fusion.14), channel_id=1, source_target_pairs={{2,0},{4,2},{6,4},{8,6},{10,8},{12,10},{14,12},{16,14},{18,16},{20... | collective-permute-start | bytes 14155784 | tf_op jit(solution)/shard_map/ppermute | solution.py:12
  109.3 10.9 %slice-start = ((s8[4718592]{0:T(1024)(128)(4,1)}), s8[524288]{0:T(1024)(128)(4,1)S(1)}, s32[]{:S(2)}) async-start(s8[4718592]{0:T(1024)(128)(4,1)} %bitcast.86), calls=%async_computation | async-start | bytes 1048576
  111.0 9.2 %slice-start.1 = ((s8[4718592]{0:T(1024)(128)(4,1)}), s8[4194304]{0:T(1024)(128)(4,1)S(1)}, s32[]{:S(2)}) async-start(s8[4718592]{0:T(1024)(128)(4,1)} %bitcast.86), calls=%async_computation.1 | async-start | bytes 8388608

commit v2 on v1

v2 whole, which is shorter than its diff:
```python
import functools
import math

import jax
import jax.numpy as jnp
from jax import lax
from jax.experimental import pallas as pl
from jax.experimental.pallas import tpu as pltpu
from jax.sharding import PartitionSpec as P

HD = 128
ROWS = 128
SCALING = HD ** (-0.5)
TO_EXP2 = SCALING * math.log2(math.e)


def from_behind(value, axis, steps):
    count = lax.axis_size(axis)
    first, last = (max(0, -steps), min(count, count - steps))
    return lax.ppermute(value, axis, [(source, source + steps) for source in range(first, last)])


def fill_bias(starts_ref, bias):
    @pl.when(pl.program_id(0) == 0)
    def _():
        token_j = lax.broadcasted_iota(jnp.int32, bias.shape, 0)
        token_i = lax.broadcasted_iota(jnp.int32, bias.shape, 1)
        allowed = (token_j <= token_i) & (token_j >= starts_ref[...])
        bias[...] = jnp.where(allowed, 0.0, -1e30)


def stacked(ref, rows, pair, together):
    columns = pl.ds(pl.multiple_of(pair * (together * HD), HD), together * HD)
    block = ref[rows, columns]
    return jnp.concatenate(
        [block[:, at * HD : (at + 1) * HD] for at in range(together)], axis=0
    )


def times(left, right, dims=((1,), (0,))):
    return lax.dot_general(left, right, (dims, ((), ())), preferred_element_type=jnp.float32)


def exponents(key_ref, query_h, bias, rows, reach, together):
    scores = times(key_ref[:reach, :], query_h, ((1,), (1,)))
    return scores * TO_EXP2 + jnp.concatenate([bias[:reach, rows]] * together, axis=1)


def softmax_kernel(
    together, starts_ref, query_ref, grad_ref, key_ref, out_ref, top_ref, inv_ref, bias, total
):
    fill_bias(starts_ref, bias)
    length = query_ref.shape[0]
    total[...] = jnp.zeros_like(total)

    @pl.loop(0, query_ref.shape[1] // (together * HD))
    def _(pair):
        for at in range(length // ROWS):
            reach = (at + 1) * ROWS
            rows = slice(at * ROWS, reach)
            query_h = stacked(query_ref, rows, pair, together)
            grad_h = stacked(grad_ref, rows, pair, together)
            power = exponents(key_ref, query_h, bias, rows, reach, together)
            top = jnp.max(power, axis=0, keepdims=True)
            expo = jnp.exp2(power - top)
            inverse = 1.0 / jnp.sum(expo, axis=0, keepdims=True)
            probs_low = (expo * inverse).astype(jnp.bfloat16)
            total[:reach, :] += times(probs_low, grad_h)
            top_ref[0, pair, at : at + 1, :] = top
            inv_ref[0, pair, at : at + 1, :] = inverse

    out_ref[...] = total[...].astype(out_ref.dtype)


def grads_kernel(
    together,
    starts_ref,
    query_ref,
    grad_ref,
    key_ref,
    value_ref,
    top_ref,
    inv_ref,
    grad_query_ref,
    grad_key_ref,
    bias,
    total,
    key_t,
):
    fill_bias(starts_ref, bias)
    length = query_ref.shape[0]
    total[...] = jnp.zeros_like(total)
    key_t[...] = key_ref[...].astype(jnp.float32).T.astype(key_t.dtype)

    @pl.loop(0, query_ref.shape[1] // (together * HD))
    def _(pair):
        for at in range(length // ROWS):
            reach = (at + 1) * ROWS
            rows = slice(at * ROWS, reach)
            query_h = stacked(query_ref, rows, pair, together)
            grad_h = stacked(grad_ref, rows, pair, together)
            power = exponents(key_ref, query_h, bias, rows, reach, together)
            top = top_ref[0, pair, at : at + 1, :]
            inverse = inv_ref[0, pair, at : at + 1, :]
            probs = jnp.exp2(power - top) * inverse
            probs_low = probs.astype(jnp.bfloat16).astype(jnp.float32)
            grad_probs = times(value_ref[:reach, :], grad_h, ((1,), (1,)))
            delta = jnp.sum(probs_low * grad_probs, axis=0, keepdims=True)
            scaled_low = (probs * (grad_probs - delta) * SCALING).astype(jnp.bfloat16)
            total[:reach, :] += times(scaled_low, query_h)
            grad_t = times(key_t[:, :reach], scaled_low)
            for head in range(together):
                columns = pl.ds(pl.multiple_of((pair * together + head) * HD, HD), HD)
                piece = grad_t[:, head * ROWS : (head + 1) * ROWS]
                grad_query_ref[rows, columns] = piece.T.astype(grad_query_ref.dtype)

    grad_key_ref[...] = total[...].astype(grad_key_ref.dtype)


def attention_calls(queries, key_rows):
    length = queries.shape[0]
    kv_heads = key_rows.shape[1] // HD
    width = queries.shape[1] // kv_heads
    groups = width // HD
    together = 2 if groups % 2 == 0 else 1
    starts_spec = pl.BlockSpec((1, length), lambda g: (0, 0))
    wide_spec = pl.BlockSpec((length, width), lambda g: (0, g))
    slim_spec = pl.BlockSpec((length, HD), lambda g: (0, g))
    stat_shape = (kv_heads, groups // together, length // ROWS, together * ROWS)
    stat_spec = pl.BlockSpec((1,) + stat_shape[1:], lambda g: (g, 0, 0, 0))
    stat = jax.ShapeDtypeStruct(stat_shape, jnp.float32)
    slim = jax.ShapeDtypeStruct(key_rows.shape, jnp.bfloat16)
    wide = jax.ShapeDtypeStruct(queries.shape, jnp.bfloat16)
    bias = pltpu.VMEM((length, length), jnp.float32)
    total = pltpu.VMEM((length, HD), jnp.float32)
    pairs = kv_heads * groups * length * length
    params = pltpu.CompilerParams(vmem_limit_bytes=32 * 2**20)
    softmax = pl.pallas_call(
        functools.partial(softmax_kernel, together),
        grid=(kv_heads,),
        in_specs=[starts_spec, wide_spec, wide_spec, slim_spec],
        out_specs=[slim_spec, stat_spec, stat_spec],
        out_shape=[slim, stat, stat],
        scratch_shapes=[bias, total],
        compiler_params=params,
        cost_estimate=pl.CostEstimate(
            flops=pairs * HD * 4, bytes_accessed=4 * queries.size, transcendentals=pairs
        ),
        name="softmax_value_grad",
    )
    grads = pl.pallas_call(
        functools.partial(grads_kernel, together),
        grid=(kv_heads,),
        in_specs=[starts_spec, wide_spec, wide_spec, slim_spec, slim_spec, stat_spec, stat_spec],
        out_specs=[wide_spec, slim_spec],
        out_shape=[wide, slim],
        scratch_shapes=[bias, total, pltpu.VMEM((HD, length), jnp.bfloat16)],
        compiler_params=params,
        cost_estimate=pl.CostEstimate(
            flops=pairs * HD * 8, bytes_accessed=6 * queries.size, transcendentals=pairs
        ),
        name="query_key_grad",
    )
    return softmax, grads


def sum_columns(terms, axis):
    count = lax.axis_size(axis)
    me = lax.axis_index(axis)
    width = terms.shape[1] // count
    total = lax.dynamic_slice_in_dim(terms, me * width, width, axis=1)
    for step in range(1, count):
        target = lax.rem(me + step, count)
        block = lax.dynamic_slice_in_dim(terms, target * width, width, axis=1)
        total = total + lax.ppermute(
            block, axis, [(source, (source + step) % count) for source in range(count)]
        )
    return total


def join_columns(block, axis):
    count = lax.axis_size(axis)
    me = lax.axis_index(axis)
    width = block.shape[1]
    whole = jnp.zeros((block.shape[0], width * count), block.dtype)
    whole = lax.dynamic_update_slice_in_dim(whole, block, me * width, axis=1)
    for step in range(1, count):
        origin = lax.rem(me + count - step, count)
        came = lax.ppermute(
            block, axis, [(source, (source + step) % count) for source in range(count)]
        )
        whole = lax.dynamic_update_slice_in_dim(whole, came, origin * width, axis=1)
    return whole


def shards(tokens_x, queries, key_rows, out_grad, value_weight, doc_starts):
    inputs = tokens_x[0]
    query_s = queries[0]
    key_s = key_rows[0]
    grad_s = out_grad[0]
    panel = value_weight[0]
    softmax, grads = attention_calls(query_s, key_s)
    grad_value, top, inverse = softmax(doc_starts, query_s, grad_s, key_s)
    grad_value, inputs = lax.optimization_barrier((grad_value, inputs))
    grad_all = join_columns(grad_value, "tensor")
    terms = jnp.dot(inputs, panel, preferred_element_type=jnp.float32)
    values = sum_columns(terms, "tensor").astype(jnp.bfloat16)
    input_grad = lax.dot_general(
        grad_all, panel, (((1,), (1,)), ((), ())), preferred_element_type=jnp.float32
    ).astype(jnp.bfloat16)
    received = from_behind(input_grad, "pipe", -1)
    grad_query, grad_key = grads(doc_starts, query_s, grad_s, key_s, values, top, inverse)
    weight_grad = lax.dot_general(
        inputs, grad_all, (((0,), (0,)), ((), ())), preferred_element_type=jnp.float32
    ).astype(jnp.bfloat16)
    return (grad_query[None], grad_key[None], weight_grad[None], received[None])


def solution(mesh):
    placed = (
        P("pipe", None, "tensor"),
        P("pipe", None, "tensor"),
        P("pipe", None, "tensor"),
        P("pipe", None, "tensor"),
        P("pipe", "tensor", None),
        P("pipe", None),
    )
    return jax.shard_map(
        shards,
        mesh=mesh,
        in_specs=placed,
        out_specs=(
            P("pipe", None, "tensor"),
            P("pipe", None, "tensor"),
            P("pipe", "tensor", None),
            P("pipe", None, "tensor"),
        ),
        check_vma=False,
    )
```

time: 171 us -> 119 us (0.70); the launches traced: 168 us -> 118 us
  matrix products: 103 us -> 32.4 us
  Pallas kernels: 0 us -> 52.4 us
  local copies, waits for them, and re-layouts: 45.4 us -> 8.83 us
  waiting for transfers between devices: 0.01 us -> 16.8 us
  other arithmetic: 13.5 us -> 0.13 us
    pallas_call x0 -> x2, Pallas kernels: none -> 52.4 us  [the longest x1 30 us: shards(): grads(doc_starts, query_s, grad_s, key_s, values, top, inverse)]
    dot_general x5 -> x0, matrix products: 48.5 us -> none  [the longest x1 16.9 us: one_group(): jnp.einsum('igd,jd->gij', grad_g, value_g, preferred_element_type=jnp.flo...]
    unnamed x18 -> x25, local copies, waits for them, and re-layouts: 42.5 us -> 8.58 us
    sub x1 -> x0, matrix products: 16.4 us -> none  [one_group(): expo = jnp.exp(scores - top_score)]
    convert_element_type x1 -> x0, other arithmetic: 11.4 us -> none  [one_group(): probs_low = probs.astype(jnp.bfloat16)]
    ppermute x1, waiting for transfers between devices: 0.01 us -> 8.7 us  [join_columns(): lax.ppermute(block, axis, [(source, (source + step) % count) for source i...]
    ppermute x1, waiting for transfers between devices: 0.01 us -> 8.1 us  [sum_columns(): lax.ppermute(block, axis, [(source, (source + step) % count) for source i...]
    dot_general x1, matrix products: 19.1 us -> 14.7 us  [shards(): lax.dot_general(grad_all, panel, (((1,), (1,)), ((), ())), preferred_elem...]
  transfers between devices with their start and end apart: 3 -> 3, of which waited for: 0 -> 2; matrix products, arithmetic and copies ran while one was open for 65% -> 15% of each run, Pallas kernels for 0% -> 25%
where the time goes in v2:
time: 119 us; the launch traced here: 118 us
  Pallas kernels  52.4 us (44%)
  matrix products  32.4 us (27%)
  waiting for transfers between devices  16.8 us (14%)
  local copies, waits for them, and re-layouts  8.83 us (7%)
  starting transfers between devices  6.76 us (6%)
    pallas_call x1, Pallas kernels, shards(): grads(doc_starts, query_s, grad_s, key_s, values, top, inverse)  30 us
    pallas_call x1, Pallas kernels, shards(): grad_value, top, inverse = softmax(doc_starts, query_s, grad_s, key_s)  22.4 us
    dot_general x1, matrix products, shards(): lax.dot_general(grad_all, panel, (((1,), (1,)), ((), ())), preferred_elem...  14.7 us
    dot_general x1, matrix products, shards(): lax.dot_general(inputs, grad_all, (((0,), (0,)), ((), ())), preferred_ele...  9.68 us
    ppermute x1, waiting for transfers between devices, join_columns(): lax.ppermute(block, axis, [(source, (source + step) % count) for source i...  8.7 us
    unnamed x25, local copies, waits for them, and re-layouts  8.58 us
    ppermute x1, waiting for transfers between devices, sum_columns(): lax.ppermute(block, axis, [(source, (source + step) % count) for source i...  8.1 us
    dot_general x1, matrix products, shards(): terms = jnp.dot(inputs, panel, preferred_element_type=jnp.float32)  8 us
  transfers between devices with their start and end apart: 3, of which 2 were waited for; matrix products, arithmetic and copies ran while one was open for 15% of the time, Pallas kernels for 25%

profile of v2, /device:TPU:1, one launch (start us, length us, event | category | flops | bytes accessed | tf_op | source)
XLA Modules:
  0.0 118.1 jit_solution(13536975709312162839)
XLA Ops:
  0.6 0.0 copy-start
  0.6 2.3 %copy-done = bf16[1,384,6144]{2,1,0:T(8,128)(2,1)S(1)} copy-done((bf16[1,384,6144]{2,1,0:T(8,128)(2,1)S(1)}, bf16[1,384,6144]{2,1,0:T(8,128)(2,1)}, u32[]{:S(2)}) %copy-start) | copy-done | bytes 4718616
  3.0 0.0 copy-start.1
  3.0 2.3 %copy-done.1 = bf16[1,384,6144]{2,1,0:T(8,128)(2,1)S(1)} copy-done((bf16[1,384,6144]{2,1,0:T(8,128)(2,1)S(1)}, bf16[1,384,6144]{2,1,0:T(8,128)(2,1)}, u32[]{:S(2)}) %copy-start.1) | copy-done | bytes 4718616
  5.3 0.0 copy-start.2
  5.3 1.0 copy-done.2
  6.3 0.0 copy-start.4
  6.3 0.7 copy-done.4
  7.0 22.4 %softmax_value_grad.1 = (bf16[384,512]{1,0:T(8,128)(2,1)S(1)}, f32[4,6,3,256]{3,2,1,0:T(4,128)S(1)}, f32[4,6,3,256]{3,2,1,0:T(4,128)S(1)}) custom-call(s32[1,384]{1,0:T(1,128)S(1)} %copy-done.4, bf16[384,6144]{1,0:T(8,128)(2,1)S(1)} %bitcast.20, bf16[384,6144]{1,0:T(8,128)(2,1)S(1)} %bitcast.24, bf16[384,512]{1,0:T(8,128)(2,1)S(1)} %bitcast.28), custom_call_target="tpu_custom_call" | custom-call | flops 3623878656 | bytes 9437184 | tf_op jit(solution)/shard_map/softmax_value_grad/pallas_call | solution.py:203
  29.4 2.1 %collective-permute-start.1 = (bf16[384,512]{1,0:T(8,128)(2,1)S(1)}, bf16[384,512]{1,0:T(8,128)(2,1)S(1)}, u32[]{:S(2)}, u32[]{:S(2)}) collective-permute-start(bf16[384,512]{1,0:T(8,128)(2,1)S(1)} %get-tuple-element.17), channel_id=1, source_target_pairs={{0,1},{1,0},{2,3},{3,2},{4,5},{5,4},{6,7},{7,6},{8,9},{9,8},{10,11... | collective-permute-start | bytes 1179656 | tf_op jit(solution)/shard_map/ppermute | solution.py:189
  31.5 0.1 broadcast_in_dim.17
  31.6 8.7 %collective-permute-done.1 = bf16[384,512]{1,0:T(8,128)(2,1)S(1)} collective-permute-done((bf16[384,512]{1,0:T(8,128)(2,1)S(1)}, bf16[384,512]{1,0:T(8,128)(2,1)S(1)}, u32[]{:S(2)}, u32[]{:S(2)}) %collective-permute-start.1) | collective-permute-done | bytes 393248 | tf_op jit(solution)/shard_map/ppermute | solution.py:189
  40.3 0.0 slice-start.4
  40.4 0.0 slice-start.5
  40.4 14.7 %fusion.4 = bf16[384,6144]{1,0:T(8,128)(2,1)} fusion(bf16[384,1024]{1,0:T(8,128)(2,1)S(1)} %constant_dynamic-update-slice_fusion, bf16[1,6144,1024]{2,1,0:T(8,128)(2,1)} %param.10), kind=kOutput, calls=%fused_computation.5 | convolution fusion | flops 4834197504 | bytes 18087936 | tf_op jit(solution)/shard_map/dot_general | solution.py:208
  55.1 3.1 %collective-permute-start.2 = (bf16[384,6144]{1,0:T(8,128)(2,1)}, bf16[384,6144]{1,0:T(8,128)(2,1)S(1)}, u32[]{:S(2)}, u32[]{:S(2)}) collective-permute-start(bf16[384,6144]{1,0:T(8,128)(2,1)} %fusion.4), channel_id=1, source_target_pairs={{2,0},{4,2},{6,4},{8,6},{10,8},{12,10},{14,12},{16,14},{18,16},{20... | collective-permute-start | bytes 14155784 | tf_op jit(solution)/shard_map/ppermute | solution.py:20
  58.2 0.0 slice-done.4
  58.2 0.0 slice-done.5
  58.2 8.0 %fusion.2 = f32[384,1024]{1,0:T(8,128)S(1)} fusion(bf16[384,6144]{1,0:T(8,128)(2,1)S(1)} %bitcast.33, bf16[1,6144,1024]{2,1,0:T(8,128)(2,1)} %param.10), kind=kOutput, calls=%fused_computation.2 | convolution fusion | flops 4831838208 | bytes 18874368 | tf_op jit(solution)/shard_map/dot_general | solution.py:206
  66.2 0.0 slice-start
  66.2 0.0 slice-start.2
  66.3 0.1 constant_dynamic-slice_fusion
  66.3 0.0 slice-start.1
  66.4 0.0 slice-start.3
  66.4 0.0 copy-start.3
  66.4 0.0 copy-start.5
  66.4 1.5 %collective-permute-start = (f32[384,512]{1,0:T(8,128)S(1)}, f32[384,512]{1,0:T(8,128)S(1)}, u32[]{:S(2)}, u32[]{:S(2)}) collective-permute-start(f32[384,512]{1,0:T(8,128)S(1)} %constant_dynamic-slice_fusion), channel_id=1, source_target_pairs={{0,1},{1,0},{2,3},{3,2},{4,5},{5,4},{6,7},{7,6},{8,9},{9,8},{10,11... | collective-permute-start | bytes 2359304 | tf_op jit(solution)/shard_map/ppermute | solution.py:175
  67.9 9.7 %convert_bitcast_fusion = bf16[1,6144,1024]{2,1,0:T(8,128)(2,1)} fusion(bf16[384,6144]{1,0:T(8,128)(2,1)S(1)} %bitcast.34, bf16[384,1024]{1,0:T(8,128)(2,1)S(1)} %constant_dynamic-update-slice_fusion), kind=kOutput, calls=%fused_computation.4 | convolution fusion | flops 4838129664 | bytes 18087936 | tf_op jit(solution)/shard_map/dot_general | solution.py:213
  77.6 8.1 %collective-permute-done = f32[384,512]{1,0:T(8,128)S(1)} collective-permute-done((f32[384,512]{1,0:T(8,128)S(1)}, f32[384,512]{1,0:T(8,128)S(1)}, u32[]{:S(2)}, u32[]{:S(2)}) %collective-permute-start) | collective-permute-done | bytes 786464 | tf_op jit(solution)/shard_map/ppermute | solution.py:175
  85.7 0.1 add_convert_fusion.value_ref
  85.8 0.0 slice-done
  85.8 0.0 slice-done.2
  85.9 0.0 slice-done.1
  85.9 0.0 slice-done.3
  85.9 0.0 copy-done.3
  85.9 0.0 copy-done.5
  85.9 30.0 %query_key_grad.1 = (bf16[384,6144]{1,0:T(8,128)(2,1)}, bf16[384,512]{1,0:T(8,128)(2,1)}) custom-call(s32[1,384]{1,0:T(1,128)S(1)} %copy-done.5, bf16[384,6144]{1,0:T(8,128)(2,1)S(1)} %bitcast.23, bf16[384,6144]{1,0:T(8,128)(2,1)S(1)} %bitcast.27, bf16[384,512]{1,0:T(8,128)(2,1)S(1)} %bitcast.29, bf16[384,512]{1,0:T(8,128)(2,1)S(1)} %add_convert_fusion.value_ref, ...), custom_call_target="tpu_custom_call" | custom-call | flops 7247757312 | bytes 14155776 | tf_op jit(solution)/shard_map/query_key_grad/pallas_call | solution.py:212
  115.9 0.0 collective-permute-done.2
  115.9 2.2 %copy.13 = bf16[1,384,6144]{2,1,0:T(8,128)(2,1)} copy(bf16[1,384,6144]{2,1,0:T(8,128)(2,1)S(1)} %bitcast.30) | data formatting | bytes 9437184
  (5 shorter events, 0.1 us)
Async XLA Ops:
  0.6 2.3 %copy-start = (bf16[1,384,6144]{2,1,0:T(8,128)(2,1)S(1)}, bf16[1,384,6144]{2,1,0:T(8,128)(2,1)}, u32[]{:S(2)}) copy-start(bf16[1,384,6144]{2,1,0:T(8,128)(2,1)} %param.7) | copy-start | bytes 14155780
  3.0 2.3 %copy-start.1 = (bf16[1,384,6144]{2,1,0:T(8,128)(2,1)S(1)}, bf16[1,384,6144]{2,1,0:T(8,128)(2,1)}, u32[]{:S(2)}) copy-start(bf16[1,384,6144]{2,1,0:T(8,128)(2,1)} %param.9) | copy-start | bytes 14155780
  5.3 1.0 copy-start.2
  6.3 0.7 copy-start.4
  29.4 10.9 %collective-permute-start.1 = (bf16[384,512]{1,0:T(8,128)(2,1)S(1)}, bf16[384,512]{1,0:T(8,128)(2,1)S(1)}, u32[]{:S(2)}, u32[]{:S(2)}) collective-permute-start(bf16[384,512]{1,0:T(8,128)(2,1)S(1)} %get-tuple-element.17), channel_id=1, source_target_pairs={{0,1},{1,0},{2,3},{3,2},{4,5},{5,4},{6,7},{7,6},{8,9},{9,8},{10,11... | collective-permute-start | bytes 1179656 | tf_op jit(solution)/shard_map/ppermute | solution.py:189
  40.3 17.9 %slice-start.4 = ((s8[4718592]{0:T(1024)(128)(4,1)}), s8[524288]{0:T(1024)(128)(4,1)S(1)}, s32[]{:S(2)}) async-start(s8[4718592]{0:T(1024)(128)(4,1)} %bitcast.31), calls=%async_computation.4 | async-start | bytes 1048576
  40.4 17.8 %slice-start.5 = ((s8[4718592]{0:T(1024)(128)(4,1)}), s8[4194304]{0:T(1024)(128)(4,1)S(1)}, s32[]{:S(2)}) async-start(s8[4718592]{0:T(1024)(128)(4,1)} %bitcast.31), calls=%async_computation.5 | async-start | bytes 8388608
  55.1 60.9 %collective-permute-start.2 = (bf16[384,6144]{1,0:T(8,128)(2,1)}, bf16[384,6144]{1,0:T(8,128)(2,1)S(1)}, u32[]{:S(2)}, u32[]{:S(2)}) collective-permute-start(bf16[384,6144]{1,0:T(8,128)(2,1)} %fusion.4), channel_id=1, source_target_pairs={{2,0},{4,2},{6,4},{8,6},{10,8},{12,10},{14,12},{16,14},{18,16},{20... | collective-permute-start | bytes 14155784 | tf_op jit(solution)/shard_map/ppermute | solution.py:20
  66.2 19.6 %slice-start = ((s8[4718592]{0:T(1024)(128)(4,1)}), s8[4194304]{0:T(1024)(128)(4,1)S(1)}, s32[]{:S(2)}) async-start(s8[4718592]{0:T(1024)(128)(4,1)} %bitcast.21), calls=%async_computation | async-start | bytes 8388608
  66.2 19.6 %slice-start.2 = ((s8[4718592]{0:T(1024)(128)(4,1)}), s8[4194304]{0:T(1024)(128)(4,1)S(1)}, s32[]{:S(2)}) async-start(s8[4718592]{0:T(1024)(128)(4,1)} %bitcast.25), calls=%async_computation.2 | async-start | bytes 8388608
  66.3 19.5 %slice-start.1 = ((s8[4718592]{0:T(1024)(128)(4,1)}), s8[524288]{0:T(1024)(128)(4,1)S(1)}, s32[]{:S(2)}) async-start(s8[4718592]{0:T(1024)(128)(4,1)} %bitcast.21), calls=%async_computation.1 | async-start | bytes 1048576
  66.4 19.5 %slice-start.3 = ((s8[4718592]{0:T(1024)(128)(4,1)}), s8[524288]{0:T(1024)(128)(4,1)S(1)}, s32[]{:S(2)}) async-start(s8[4718592]{0:T(1024)(128)(4,1)} %bitcast.25), calls=%async_computation.3 | async-start | bytes 1048576
  66.4 19.5 %copy-start.3 = (bf16[1,384,512]{2,1,0:T(8,128)(2,1)S(1)}, bf16[1,384,512]{2,1,0:T(8,128)(2,1)}, u32[]{:S(2)}) copy-start(bf16[1,384,512]{2,1,0:T(8,128)(2,1)} %param.8) | copy-start | bytes 1179652
  66.4 19.5 %copy-start.5 = (s32[1,384]{1,0:T(1,128)S(1)}, s32[1,384]{1,0:T(1,128)}, u32[]{:S(2)}) copy-start(s32[1,384]{1,0:T(1,128)} %starts_ref.3) | copy-start | bytes 4612
  66.4 19.3 %collective-permute-start = (f32[384,512]{1,0:T(8,128)S(1)}, f32[384,512]{1,0:T(8,128)S(1)}, u32[]{:S(2)}, u32[]{:S(2)}) collective-permute-start(f32[384,512]{1,0:T(8,128)S(1)} %constant_dynamic-slice_fusion), channel_id=1, source_target_pairs={{0,1},{1,0},{2,3},{3,2},{4,5},{5,4},{6,7},{7,6},{8,9},{9,8},{10,11... | collective-permute-start | bytes 2359304 | tf_op jit(solution)/shard_map/ppermute | solution.py:175

commit v3 on v2

--- a/solution.py
+++ b/solution.py
@@ -10,6 +10,7 @@
 
 HD = 128
 ROWS = 128
+PARTS = 2
 SCALING = HD ** (-0.5)
 TO_EXP2 = SCALING * math.log2(math.e)
 
@@ -53,9 +54,12 @@
     length = query_ref.shape[0]
     total[...] = jnp.zeros_like(total)
 
-    @pl.loop(0, query_ref.shape[1] // (together * HD))
-    def _(pair):
-        for at in range(length // ROWS):
+    pairs = query_ref.shape[1] // (together * HD)
+    unroll = math.gcd(pairs, 6)
+
+    @pl.loop(0, pairs, step=unroll)
+    def _(first):
+        for at, pair in [(a, first + u) for a in range(length // ROWS) for u in range(unroll)]:
             reach = (at + 1) * ROWS
             rows = slice(at * ROWS, reach)
             query_h = stacked(query_ref, rows, pair, together)
@@ -92,9 +96,12 @@
     total[...] = jnp.zeros_like(total)
     key_t[...] = key_ref[...].astype(jnp.float32).T.astype(key_t.dtype)
 
-    @pl.loop(0, query_ref.shape[1] // (together * HD))
-    def _(pair):
-        for at in range(length // ROWS):
+    pairs = query_ref.shape[1] // (together * HD)
+    unroll = math.gcd(pairs, 6)
+
+    @pl.loop(0, pairs, step=unroll)
+    def _(first):
+        for at, pair in [(a, first + u) for a in range(length // ROWS) for u in range(unroll)]:
             reach = (at + 1) * ROWS
             rows = slice(at * ROWS, reach)
             query_h = stacked(query_ref, rows, pair, together)
@@ -134,7 +141,7 @@
     bias = pltpu.VMEM((length, length), jnp.float32)
     total = pltpu.VMEM((length, HD), jnp.float32)
     pairs = kv_heads * groups * length * length
-    params = pltpu.CompilerParams(vmem_limit_bytes=32 * 2**20)
+    params = pltpu.CompilerParams(vmem_limit_bytes=56 * 2**20)
     softmax = pl.pallas_call(
         functools.partial(softmax_kernel, together),
         grid=(kv_heads,),
@@ -204,11 +211,15 @@
     grad_value, inputs = lax.optimization_barrier((grad_value, inputs))
     grad_all = join_columns(grad_value, "tensor")
     terms = jnp.dot(inputs, panel, preferred_element_type=jnp.float32)
+    grad_all, terms = lax.optimization_barrier((grad_all, terms))
     values = sum_columns(terms, "tensor").astype(jnp.bfloat16)
-    input_grad = lax.dot_general(
-        grad_all, panel, (((1,), (1,)), ((), ())), preferred_element_type=jnp.float32
-    ).astype(jnp.bfloat16)
-    received = from_behind(input_grad, "pipe", -1)
+    came = []
+    for part in jnp.split(panel, PARTS, axis=0):
+        input_grad = lax.dot_general(
+            grad_all, part, (((1,), (1,)), ((), ())), preferred_element_type=jnp.float32
+        ).astype(jnp.bfloat16)
+        came.append(from_behind(input_grad, "pipe", -1))
+    received = jnp.concatenate(came, axis=1)
     grad_query, grad_key = grads(doc_starts, query_s, grad_s, key_s, values, top, inverse)
     weight_grad = lax.dot_general(
         inputs, grad_all, (((0,), (0,)), ((), ())), preferred_element_type=jnp.float32

time: 119 us -> 94.8 us (0.80)
  Pallas kernels: 52.4 us -> 37.9 us
  local copies, waits for them, and re-layouts: 8.83 us -> 0.25 us
  waiting for transfers between devices: 16.8 us -> 11.1 us
  other arithmetic: 0.13 us -> 3.46 us
  starting transfers between devices: 6.76 us -> 8.85 us
    pallas_call x1, Pallas kernels: 22.4 us -> 11.4 us  [shards(): grad_value, top, inverse = softmax(doc_starts, query_s, grad_s, key_s)]
    unnamed x25 -> x6, local copies, waits for them, and re-layouts: 8.58 us -> 0.02 us
    ppermute x1, waiting for transfers between devices: 8.7 us -> 0.87 us  [join_columns(): lax.ppermute(block, axis, [(source, (source + step) % count) for source i...]
    ppermute x1 -> x2, waiting for transfers between devices: 0.01 us -> 5.22 us  [from_behind(): lax.ppermute(value, axis, [(source, source + steps) for source in range(f...]
    pallas_call x1, Pallas kernels: 30 us -> 26.5 us  [shards(): grads(doc_starts, query_s, grad_s, key_s, values, top, inverse)]
    ppermute x1, waiting for transfers between devices: 8.1 us -> 4.99 us  [sum_columns(): lax.ppermute(block, axis, [(source, (source + step) % count) for source i...]
    broadcast_in_dim x0 -> x1, other arithmetic: none -> 2.59 us  [shards(): return (grad_query[None], grad_key[None], weight_grad[None], received[None])]
    dot_general x1, matrix products: 9.68 us -> 12 us  [shards(): lax.dot_general(inputs, grad_all, (((0,), (0,)), ((), ())), preferred_ele...]
  transfers between devices with their start and end apart: 3 -> 4, of which waited for: 2 -> 3; matrix products, arithmetic and copies ran while one was open for 15% -> 22% of each run, Pallas kernels for 25% -> 28%
where the time goes in v3:
time: 94.8 us; the launch traced here: 94.7 us
  Pallas kernels  37.9 us (40%)
  matrix products  32.3 us (34%)
  waiting for transfers between devices  11.1 us (12%)
  starting transfers between devices  8.85 us (9%)
  other arithmetic  3.46 us (4%)
    pallas_call x1, Pallas kernels, shards(): grads(doc_starts, query_s, grad_s, key_s, values, top, inverse)  26.5 us
    dot_general x2, matrix products, shards(): lax.dot_general(grad_all, part, (((1,), (1,)), ((), ())), preferred_eleme...  12.3 us
    dot_general x1, matrix products, shards(): lax.dot_general(inputs, grad_all, (((0,), (0,)), ((), ())), preferred_ele...  12 us
    pallas_call x1, Pallas kernels, shards(): grad_value, top, inverse = softmax(doc_starts, query_s, grad_s, key_s)  11.4 us
    dot_general x1, matrix products, shards(): terms = jnp.dot(inputs, panel, preferred_element_type=jnp.float32)  7.99 us
    ppermute x2, starting transfers between devices, from_behind(): lax.ppermute(value, axis, [(source, source + steps) for source in range(f...  5.23 us
    ppermute x2, waiting for transfers between devices, from_behind(): lax.ppermute(value, axis, [(source, source + steps) for source in range(f...  5.22 us
    ppermute x1, waiting for transfers between devices, sum_columns(): lax.ppermute(block, axis, [(source, (source + step) % count) for source i...  4.99 us
  transfers between devices with their start and end apart: 4, of which 3 were waited for; matrix products, arithmetic and copies ran while one was open for 22% of the time, Pallas kernels for 28%

profile of v3, /device:TPU:1, one launch (start us, length us, event | category | flops | bytes accessed | tf_op | source)
XLA Modules:
  0.0 94.7 jit_solution(6130626882203812554)
XLA Ops:
  0.6 0.0 copy-start.2
  0.6 11.4 %softmax_value_grad.1 = (bf16[384,512]{1,0:T(8,128)(2,1)}, f32[4,6,3,256]{3,2,1,0:T(4,128)}, f32[4,6,3,256]{3,2,1,0:T(4,128)}) custom-call(s32[1,384]{1,0:T(1,128)} %starts_ref.3, bf16[384,6144]{1,0:T(8,128)(2,1)} %bitcast.30, bf16[384,6144]{1,0:T(8,128)(2,1)} %bitcast.32, bf16[384,512]{1,0:T(8,128)(2,1)} %bitcast.34), custom_call_target="tpu_custom_call" | custom-call | flops 3623878656 | bytes 9437184 | tf_op jit(solution)/shard_map/softmax_value_grad/pallas_call | solution.py:210
  12.0 0.0 copy-start
  12.0 2.1 %collective-permute-start = (bf16[384,512]{1,0:T(8,128)(2,1)}, bf16[384,512]{1,0:T(8,128)(2,1)S(1)}, u32[]{:S(2)}, u32[]{:S(2)}) collective-permute-start(bf16[384,512]{1,0:T(8,128)(2,1)} %get-tuple-element.14), channel_id=1, source_target_pairs={{0,1},{1,0},{2,3},{3,2},{4,5},{5,4},{6,7},{7,6},{8,9},{9,8},{10,11... | collective-permute-start | bytes 1179656 | tf_op jit(solution)/shard_map/ppermute | solution.py:196
  14.1 0.0 copy-done.2
  14.1 8.0 %fusion = f32[384,1024]{1,0:T(8,128)S(1)} fusion(bf16[384,6144]{1,0:T(8,128)(2,1)S(1)} %bitcast.29, bf16[1,6144,1024]{2,1,0:T(8,128)(2,1)} %param.10), kind=kOutput, calls=%fused_computation | convolution fusion | flops 4831838208 | bytes 18874368 | tf_op jit(solution)/shard_map/dot_general | solution.py:213
  22.1 0.1 broadcast_in_dim.15
  22.2 0.0 copy-done
  22.3 0.9 collective-permute-done
  23.2 0.0 copy-start.1
  23.2 8.4 %fusion.8 = bf16[384,3072]{1,0:T(8,128)(2,1)} fusion(bf16[384,1024]{1,0:T(8,128)(2,1)S(1)} %constant_dynamic-update-slice_fusion, bf16[1,6144,1024]{2,1,0:T(8,128)(2,1)} %param.10), kind=kOutput, calls=%fused_computation.10 | convolution fusion | flops 2417098752 | bytes 9437184 | tf_op jit(solution)/shard_map/dot_general | solution.py:218
  31.7 0.0 copy-done.1
  31.7 3.9 %fusion.11 = bf16[384,3072]{1,0:T(8,128)(2,1)} fusion(bf16[384,1024]{1,0:T(8,128)(2,1)S(1)} %constant_dynamic-update-slice_fusion, bf16[1,6144,1024]{2,1,0:T(8,128)(2,1)S(1)} %copy-done.1), kind=kOutput, calls=%fused_computation.11 | convolution fusion | flops 2417098752 | bytes 9437184 | tf_op jit(solution)/shard_map/dot_general | solution.py:218
  35.5 3.1 %collective-permute-start.2 = (bf16[384,3072]{1,0:T(8,128)(2,1)}, bf16[384,3072]{1,0:T(8,128)(2,1)S(1)}, u32[]{:S(2)}, u32[]{:S(2)}) collective-permute-start(bf16[384,3072]{1,0:T(8,128)(2,1)} %fusion.8), channel_id=1, source_target_pairs={{2,0},{4,2},{6,4},{8,6},{10,8},{12,10},{14,12},{16,14},{18,16},{20... | collective-permute-start | bytes 7077896 | tf_op jit(solution)/shard_map/ppermute | solution.py:21
  38.7 2.1 %collective-permute-start.3 = (bf16[384,3072]{1,0:T(8,128)(2,1)}, bf16[384,3072]{1,0:T(8,128)(2,1)S(1)}, u32[]{:S(2)}, u32[]{:S(2)}) collective-permute-start(bf16[384,3072]{1,0:T(8,128)(2,1)} %fusion.11), channel_id=1, source_target_pairs={{2,0},{4,2},{6,4},{8,6},{10,8},{12,10},{14,12},{16,14},{18,16},{20... | collective-permute-start | bytes 7077896 | tf_op jit(solution)/shard_map/ppermute | solution.py:21
  40.8 0.1 constant_dynamic-slice_fusion
  40.9 1.5 %collective-permute-start.1 = (f32[384,512]{1,0:T(8,128)S(1)}, f32[384,512]{1,0:T(8,128)S(1)}, u32[]{:S(2)}, u32[]{:S(2)}) collective-permute-start(f32[384,512]{1,0:T(8,128)S(1)} %constant_dynamic-slice_fusion), channel_id=1, source_target_pairs={{0,1},{1,0},{2,3},{3,2},{4,5},{5,4},{6,7},{7,6},{8,9},{9,8},{10,11... | collective-permute-start | bytes 2359304 | tf_op jit(solution)/shard_map/ppermute | solution.py:182
  42.4 12.0 %convert_bitcast_fusion = bf16[1,6144,1024]{2,1,0:T(8,128)(2,1)} fusion(bf16[384,6144]{1,0:T(8,128)(2,1)} %bitcast.28, bf16[384,1024]{1,0:T(8,128)(2,1)S(1)} %constant_dynamic-update-slice_fusion), kind=kOutput, calls=%fused_computation.2 | convolution fusion | flops 4838129664 | bytes 18087936 | tf_op jit(solution)/shard_map/dot_general | solution.py:224
  54.4 5.0 %collective-permute-done.1 = f32[384,512]{1,0:T(8,128)S(1)} collective-permute-done((f32[384,512]{1,0:T(8,128)S(1)}, f32[384,512]{1,0:T(8,128)S(1)}, u32[]{:S(2)}, u32[]{:S(2)}) %collective-permute-start.1) | collective-permute-done | bytes 786464 | tf_op jit(solution)/shard_map/ppermute | solution.py:182
  59.4 0.9 add_convert_fusion.value_ref
  60.3 26.5 %query_key_grad.1 = (bf16[384,6144]{1,0:T(8,128)(2,1)}, bf16[384,512]{1,0:T(8,128)(2,1)}) custom-call(s32[1,384]{1,0:T(1,128)} %starts_ref.3, bf16[384,6144]{1,0:T(8,128)(2,1)} %bitcast.31, bf16[384,6144]{1,0:T(8,128)(2,1)} %bitcast.33, bf16[384,512]{1,0:T(8,128)(2,1)} %bitcast.35, bf16[384,512]{1,0:T(8,128)(2,1)} %add_convert_fusion.value_ref, ...), custom_call_target="tpu_custom_call" | custom-call | flops 7247757312 | bytes 14155776 | tf_op jit(solution)/shard_map/query_key_grad/pallas_call | solution.py:223
  86.8 0.0 collective-permute-done.2
  86.9 5.2 %collective-permute-done.3 = bf16[384,3072]{1,0:T(8,128)(2,1)S(1)} collective-permute-done((bf16[384,3072]{1,0:T(8,128)(2,1)}, bf16[384,3072]{1,0:T(8,128)(2,1)S(1)}, u32[]{:S(2)}, u32[]{:S(2)}) %collective-permute-start.3) | collective-permute-done | bytes 2359328 | tf_op jit(solution)/shard_map/ppermute | solution.py:21
  92.1 2.6 %maximum_bitcast_fusion = bf16[1,384,6144]{2,1,0:T(8,128)(2,1)} fusion(bf16[384,3072]{1,0:T(8,128)(2,1)S(1)} %collective-permute-done.3, bf16[384,3072]{1,0:T(8,128)(2,1)S(1)} %collective-permute-done.2), kind=kLoop, calls=%fused_computation.9 | loop fusion | flops 9437184 | bytes 9437184 | tf_op jit(solution)/shard_map/broadcast_in_dim | solution.py:227
  (2 shorter events, 0.1 us)
Async XLA Ops:
  0.6 13.5 %copy-start.2 = (bf16[1,384,6144]{2,1,0:T(8,128)(2,1)S(1)}, bf16[1,384,6144]{2,1,0:T(8,128)(2,1)}, u32[]{:S(2)}) copy-start(bf16[1,384,6144]{2,1,0:T(8,128)(2,1)} %param.6) | copy-start | bytes 14155780
  12.0 10.2 %copy-start = (bf16[384,512]{1,0:T(8,128)(2,1)S(1)}, bf16[384,512]{1,0:T(8,128)(2,1)}, u32[]{:S(2)}) copy-start(bf16[384,512]{1,0:T(8,128)(2,1)} %get-tuple-element.14) | copy-start | bytes 1179652
  12.0 11.1 %collective-permute-start = (bf16[384,512]{1,0:T(8,128)(2,1)}, bf16[384,512]{1,0:T(8,128)(2,1)S(1)}, u32[]{:S(2)}, u32[]{:S(2)}) collective-permute-start(bf16[384,512]{1,0:T(8,128)(2,1)} %get-tuple-element.14), channel_id=1, source_target_pairs={{0,1},{1,0},{2,3},{3,2},{4,5},{5,4},{6,7},{7,6},{8,9},{9,8},{10,11... | collective-permute-start | bytes 1179656 | tf_op jit(solution)/shard_map/ppermute | solution.py:196
  23.2 8.5 %copy-start.1 = (bf16[1,6144,1024]{2,1,0:T(8,128)(2,1)S(1)}, bf16[1,6144,1024]{2,1,0:T(8,128)(2,1)}, u32[]{:S(2)}) copy-start(bf16[1,6144,1024]{2,1,0:T(8,128)(2,1)} %param.10) | copy-start | bytes 37748740
  35.5 51.3 %collective-permute-start.2 = (bf16[384,3072]{1,0:T(8,128)(2,1)}, bf16[384,3072]{1,0:T(8,128)(2,1)S(1)}, u32[]{:S(2)}, u32[]{:S(2)}) collective-permute-start(bf16[384,3072]{1,0:T(8,128)(2,1)} %fusion.8), channel_id=1, source_target_pairs={{2,0},{4,2},{6,4},{8,6},{10,8},{12,10},{14,12},{16,14},{18,16},{20... | collective-permute-start | bytes 7077896 | tf_op jit(solution)/shard_map/ppermute | solution.py:21
  38.7 53.4 %collective-permute-start.3 = (bf16[384,3072]{1,0:T(8,128)(2,1)}, bf16[384,3072]{1,0:T(8,128)(2,1)S(1)}, u32[]{:S(2)}, u32[]{:S(2)}) collective-permute-start(bf16[384,3072]{1,0:T(8,128)(2,1)} %fusion.11), channel_id=1, source_target_pairs={{2,0},{4,2},{6,4},{8,6},{10,8},{12,10},{14,12},{16,14},{18,16},{20... | collective-permute-start | bytes 7077896 | tf_op jit(solution)/shard_map/ppermute | solution.py:21
  40.9 18.5 %collective-permute-start.1 = (f32[384,512]{1,0:T(8,128)S(1)}, f32[384,512]{1,0:T(8,128)S(1)}, u32[]{:S(2)}, u32[]{:S(2)}) collective-permute-start(f32[384,512]{1,0:T(8,128)S(1)} %constant_dynamic-slice_fusion), channel_id=1, source_target_pairs={{0,1},{1,0},{2,3},{3,2},{4,5},{5,4},{6,7},{7,6},{8,9},{9,8},{10,11... | collective-permute-start | bytes 2359304 | tf_op jit(solution)/shard_map/ppermute | solution.py:182
